TPU v7x, 32 devices: a whole 2x2x4 slice. The times are simulated.
32 devices in a mesh: dp: 16 (over z, y, x), space: 2 (over core).
Axes of the slice: x: 2, y: 2, z: 4, core: 2. Of those that a mesh axis runs over, the one named last changes fastest.
Arguments:
- images: bfloat16 [16, 16, 288, 256], P('dp', 'space'), may hold values from -12 to 12
- w_reduce: bfloat16 [256, 64], replicated, may hold values from -0.375 to 0.375
- w_dilated: bfloat16 [3, 3, 64, 64], replicated, may hold values from -0.25 to 0.25
- w_expand: bfloat16 [64, 256], replicated, may hold values from -0.75 to 0.75
- gain_one: float32 [64], replicated, may hold values from 0.25 to 1.75
- shift_one: float32 [64], replicated, may hold values from -3 to 3
- gain_two: float32 [64], replicated, may hold values from 0.25 to 1.75
- shift_two: float32 [64], replicated, may hold values from -3 to 3
- gain_three: float32 [256], replicated, may hold values from 0.25 to 1.75
- shift_three: float32 [256], replicated, may hold values from -3 to 3
- cotangent: bfloat16 [16, 16, 288, 256], P('dp', 'space'), may hold values from -6 to 6
Outputs:
- result: bfloat16 [16, 16, 288, 256], P('dp', 'space')
- grad_images: bfloat16 [16, 16, 288, 256], P('dp', 'space')
- grad_reduce: float32 [256, 64], replicated
- grad_dilated: float32 [3, 3, 64, 64], replicated
- grad_expand: float32 [64, 256], replicated
- grad_gain_one: float32 [64], replicated
- grad_shift_one: float32 [64], replicated
- grad_gain_two: float32 [64], replicated
- grad_shift_two: float32 [64], replicated
- grad_gain_three: float32 [256], replicated
- grad_shift_three: float32 [256], replicated
All inputs are finite; a program needn't handle non-finite values.
Results may differ from a plain program's by a relative error of at most 0.012.
Values may be sent and summed in bfloat16 or wider, within the bound.
No kernel may reach another device: no remote copies, remote signals or barrier semaphores. Data moves between devices by JAX's collectives and lax.ppermute only.
A program may use at most 64 MiB of HBM per device.

v0:
```python
import jax
import jax.numpy as jnp
from jax import lax
from jax.sharding import PartitionSpec as P

epsilon = 1e-05


def extended(block, sides, width):
    for axis, dim in sides:
        count = lax.axis_size(axis)
        forward = [(i, i + 1) for i in range(count - 1)]
        backward = [(target, source) for source, target in forward]
        low = lax.ppermute(
            lax.slice_in_dim(block, block.shape[dim] - width, None, axis=dim), axis, forward
        )
        high = lax.ppermute(lax.slice_in_dim(block, 0, width, axis=dim), axis, backward)
        block = jnp.concatenate([low, block, high], axis=dim)
    return block


def smooth_act(value):
    return value * jax.nn.sigmoid(value)


def smooth_slope(value):
    sig = jax.nn.sigmoid(value)
    return sig * (1.0 + value * (1.0 - sig))


def normalize(pre, gain, shift, count):
    average = lax.psum(jnp.sum(pre, 0), "space") / count
    centred = pre - average
    variance = lax.psum(jnp.sum(centred * centred, 0), "space") / count
    inv_std = lax.rsqrt(variance + epsilon)
    normed = centred * inv_std
    return (normed, inv_std, gain * normed + shift)


def backnorm(grad, normed, inv_std, gain, count):
    local_sum = jnp.sum(grad, 0)
    local_cross = jnp.sum(grad * normed, 0)
    grad_sum, grad_cross = lax.psum((local_sum, local_cross), "space")
    back = (gain * inv_std * (grad - grad_sum / count - normed * grad_cross / count)).astype(
        jnp.bfloat16
    )
    return (back, local_cross, local_sum)


def dilated(padded, kernel, rows, cols):
    output = jnp.zeros((rows * cols, kernel.shape[3]), jnp.float32)
    for tap_row in range(3):
        for tap_col in range(3):
            window = padded[
                2 * tap_row : 2 * tap_row + rows, 2 * tap_col : 2 * tap_col + cols
            ].reshape(rows * cols, -1)
            output = output + jnp.dot(
                window, kernel[tap_row, tap_col], preferred_element_type=jnp.float32
            )
    return output


def contract(left, right):
    return lax.dot_general(
        left, right, (((0,), (0,)), ((), ())), preferred_element_type=jnp.float32
    )


def shards(
    images,
    w_reduce,
    w_dilated,
    w_expand,
    gain_one,
    shift_one,
    gain_two,
    shift_two,
    gain_three,
    shift_three,
    cotangent,
):
    rows, cols, chans = (images.shape[1], images.shape[2], images.shape[3])
    mids = w_reduce.shape[1]
    pixels = rows * cols
    count = float(pixels * lax.axis_size("space"))
    flat_in = images.reshape(pixels, chans)
    pre_one = jnp.dot(flat_in, w_reduce, preferred_element_type=jnp.float32)
    normed_one, istd_one, out_one = normalize(pre_one, gain_one, shift_one, count)
    act_one = smooth_act(out_one).astype(jnp.bfloat16)
    edged_one = extended(act_one.reshape(rows, cols, mids), (("space", 0),), 2)
    padded_one = jnp.pad(edged_one, ((0, 0), (2, 2), (0, 0)))
    pre_two = dilated(padded_one, w_dilated, rows, cols)
    normed_two, istd_two, out_two = normalize(pre_two, gain_two, shift_two, count)
    act_two = smooth_act(out_two).astype(jnp.bfloat16)
    pre_three = jnp.dot(act_two, w_expand, preferred_element_type=jnp.float32)
    normed_three, istd_three, out_three = normalize(pre_three, gain_three, shift_three, count)
    summed = out_three + flat_in.astype(jnp.float32)
    result = smooth_act(summed).astype(jnp.bfloat16)
    grad_three = cotangent.reshape(pixels, chans).astype(jnp.float32) * smooth_slope(summed)
    dh_three, gg_three, gs_three = backnorm(grad_three, normed_three, istd_three, gain_three, count)
    gw_expand = contract(act_two, dh_three)
    back_two = lax.dot_general(
        dh_three, w_expand, (((1,), (1,)), ((), ())), preferred_element_type=jnp.float32
    )
    grad_two = back_two * smooth_slope(out_two)
    dh_two, gg_two, gs_two = backnorm(grad_two, normed_two, istd_two, gain_two, count)
    taps = []
    for tap_row in range(3):
        for tap_col in range(3):
            window = padded_one[
                2 * tap_row : 2 * tap_row + rows, 2 * tap_col : 2 * tap_col + cols
            ].reshape(pixels, mids)
            taps.append(contract(window, dh_two))
    gw_dilated = jnp.stack(taps).reshape(3, 3, mids, mids)
    edged_back = extended(dh_two.reshape(rows, cols, mids), (("space", 0),), 2)
    padded_back = jnp.pad(edged_back, ((0, 0), (2, 2), (0, 0)))
    flipped = jnp.transpose(w_dilated[::-1, ::-1], (0, 1, 3, 2))
    grad_one = dilated(padded_back, flipped, rows, cols) * smooth_slope(out_one)
    dh_one, gg_one, gs_one = backnorm(grad_one, normed_one, istd_one, gain_one, count)
    gw_reduce = contract(flat_in, dh_one)
    back_in = lax.dot_general(
        dh_one, w_reduce, (((1,), (1,)), ((), ())), preferred_element_type=jnp.float32
    )
    grad_images = (back_in + grad_three).astype(jnp.bfloat16).reshape(1, rows, cols, chans)
    batch = float(lax.axis_size("dp"))
    parts_list = (
        gw_reduce,
        gw_dilated,
        gw_expand,
        gg_one,
        gs_one,
        gg_two,
        gs_two,
        gg_three,
        gs_three,
    )
    flat_grads = jnp.concatenate([item.reshape(-1) for item in parts_list])
    length = flat_grads.shape[0]
    groups = lax.axis_size("space")
    padded_len = (length + groups - 1) // groups * groups
    flat_grads = jnp.pad(flat_grads, (0, padded_len - length))
    share = lax.psum_scatter(
        flat_grads.astype(jnp.bfloat16), "space", scatter_dimension=0, tiled=True
    ).astype(jnp.float32)
    share = lax.psum(share, "dp")
    whole = lax.all_gather(share.astype(jnp.bfloat16), "space", axis=0, tiled=True).astype(
        share.dtype
    )
    summed_parts = []
    offset = 0
    for item in parts_list:
        summed_parts.append(whole[offset : offset + item.size].reshape(item.shape))
        offset = offset + item.size
    grads = [item / batch for item in summed_parts]
    return (
        result.reshape(1, rows, cols, chans),
        grad_images,
        grads[0],
        grads[1],
        grads[2],
        grads[3],
        grads[4],
        grads[5],
        grads[6],
        grads[7],
        grads[8],
    )


def solution(mesh):
    placed = (
        P("dp", "space", None, None),
        P(),
        P(),
        P(),
        P(),
        P(),
        P(),
        P(),
        P(),
        P(),
        P("dp", "space", None, None),
    )
    return jax.shard_map(
        shards,
        mesh=mesh,
        in_specs=placed,
        out_specs=(
            P("dp", "space", None, None),
            P("dp", "space", None, None),
            P(),
            P(),
            P(),
            P(),
            P(),
            P(),
            P(),
            P(),
            P(),
        ),
        check_vma=False,
    )
```

profile of v0, /device:TPU:0, one launch (start us, length us, event | category | flops | bytes accessed | tf_op | source)
XLA Modules:
  0.0 222.0 jit_solution(6507126635642277111)
XLA Ops:
  7.3 1.9 fusion.59
  9.2 2.6 %psum.91 = f32[64]{0:T(128)S(1)} all-reduce(f32[64]{0:T(128)S(1)} %get-tuple-element.81), channel_id=1, replica_groups=mesh['dp'=16,'space'=2] {'space'}, use_global_device_ids=true, to_apply=%region_1.0 | all-reduce | flops 64 | bytes 512 | tf_op jit(solution)/shard_map/psum | solution.py:32
  12.1 2.5 %psum.92 = f32[64]{0:T(128)S(1)} all-reduce(f32[64]{0:T(128)S(1)} %multiply_reduce_fusion.5), channel_id=1, replica_groups=mesh['dp'=16,'space'=2] {'space'}, use_global_device_ids=true, to_apply=%region_3.0 | all-reduce | flops 64 | bytes 512 | tf_op jit(solution)/shard_map/psum | solution.py:34
  16.3 2.3 %collective-permute-start = (bf16[2,288,64]{1,0,2:T(2,128)(2,1)S(1)}, bf16[2,288,64]{1,0,2:T(2,128)(2,1)S(1)}, u32[]{:S(2)}, u32[]{:S(2)}) collective-permute-start(bf16[2,288,64]{1,0,2:T(2,128)(2,1)S(1)} %slice.191), channel_id=1, source_target_pairs={{0,1},{2,3},{4,5},{6,7},{8,9},{10,11},{12,13},{14,15},{16,17},{18,... | collective-permute-start | bytes 221192 | tf_op jit(solution)/shard_map/ppermute | solution.py:14
  23.6 1.8 fusion.56
  27.5 1.4 reshape.163
  28.9 1.4 reshape.164
  34.6 1.3 reshape.165
  37.6 1.3 reshape.167
  42.2 3.3 %psum.93 = f32[64]{0:T(128)S(1)} all-reduce(f32[64]{0:T(128)S(1)} %get-tuple-element.83), channel_id=1, replica_groups=mesh['dp'=16,'space'=2] {'space'}, use_global_device_ids=true, to_apply=%region_5.6 | all-reduce | flops 64 | bytes 512 | tf_op jit(solution)/shard_map/psum | solution.py:32
  45.7 2.5 %psum.94 = f32[64]{0:T(128)S(1)} all-reduce(f32[64]{0:T(128)S(1)} %multiply_reduce_fusion.4), channel_id=1, replica_groups=mesh['dp'=16,'space'=2] {'space'}, use_global_device_ids=true, to_apply=%region_7.8 | all-reduce | flops 64 | bytes 512 | tf_op jit(solution)/shard_map/psum | solution.py:34
  48.2 1.9 fusion.61
  50.1 2.5 %psum.95 = f32[256]{0:T(256)S(1)} all-reduce(f32[256]{0:T(256)S(1)} %get-tuple-element.85), channel_id=1, replica_groups=mesh['dp'=16,'space'=2] {'space'}, use_global_device_ids=true, to_apply=%region_9.10 | all-reduce | flops 256 | bytes 2048 | tf_op jit(solution)/shard_map/psum | solution.py:32
  52.9 2.6 %psum.96 = f32[256]{0:T(256)S(1)} all-reduce(f32[256]{0:T(256)S(1)} %multiply_reduce_fusion.1), channel_id=1, replica_groups=mesh['dp'=16,'space'=2] {'space'}, use_global_device_ids=true, to_apply=%region_11.12 | all-reduce | flops 256 | bytes 2048 | tf_op jit(solution)/shard_map/psum | solution.py:34
  55.6 5.1 %fusion.52 = (f32[256]{0:T(256)S(1)}, f32[256]{0:T(256)S(1)}, f32[2304,256]{1,0:T(8,128)}, bf16[2304,256]{1,0:T(8,128)(2,1)}) fusion(f32[256]{0:T(256)S(1)} %get-tuple-element.76, f32[2304,256]{1,0:T(8,128)S(1)} %get-tuple-element.86, f32[256]{0:T(256)S(1)} %broadcast_multiply_fusion.1, bf16[1,8,288,256]{3,2,1,0:T(8,128)(2,1)} %param.11, ...), kind=kLoop, calls=%fused_computation.141 | loop fusion | flops 11795968 | bytes 8263680 | tf_op jit(solution)/shard_map/reduce_sum | solution.py:41
  60.6 2.5 %all-reduce.5 = (f32[256]{0:T(256)S(1)}, f32[256]{0:T(256)S(1)}) all-reduce(f32[256]{0:T(256)S(1)} %get-tuple-element.34, f32[256]{0:T(256)S(1)} %get-tuple-element.33), channel_id=1, replica_groups=mesh['dp'=16,'space'=2] {'space'}, use_global_device_ids=true, to_apply=%region_15.16 | all-reduce | flops 512 | bytes 4096 | tf_op jit(solution)/shard_map/psum | solution.py:43
  63.1 2.3 %multiply_convert_fusion = bf16[2304,256]{1,0:T(8,128)(2,1)S(1)} fusion(f32[2304,256]{1,0:T(8,128)} %get-tuple-element.45, f32[2304,256]{1,0:T(8,128)S(1)} %get-tuple-element.86, f32[256]{0:T(256)S(1)} %get-tuple-element.43, f32[256]{0:T(256)S(1)} %broadcast_multiply_fusion, f32[256]{0:T(256)S(1)} %get-tuple-element.75, f32[256]{0:T(256)S(1)} %get-tuple-element.76, ...), kind=kLoop, calls=%fused_computation.23 | loop fusion | flops 4718592 | bytes 5903360 | tf_op jit(solution)/shard_map/convert_element_type | solution.py:44
  65.8 1.4 fusion.54
  67.3 2.6 %all-reduce.4 = (f32[64]{0:T(128)S(1)}, f32[64]{0:T(128)S(1)}) all-reduce(f32[64]{0:T(128)S(1)} %get-tuple-element.38, f32[64]{0:T(128)S(1)} %get-tuple-element.37), channel_id=1, replica_groups=mesh['dp'=16,'space'=2] {'space'}, use_global_device_ids=true, to_apply=%region_19.20 | all-reduce | flops 128 | bytes 1024 | tf_op jit(solution)/shard_map/psum | solution.py:43
  69.9 1.5 multiply_convert_fusion.3
  73.6 2.3 %collective-permute-start.2 = (bf16[2,288,64]{1,0,2:T(2,128)(2,1)S(1)}, bf16[2,288,64]{1,0,2:T(2,128)(2,1)S(1)}, u32[]{:S(2)}, u32[]{:S(2)}) collective-permute-start(bf16[2,288,64]{1,0,2:T(2,128)(2,1)S(1)} %slice.212), channel_id=1, source_target_pairs={{0,1},{2,3},{4,5},{6,7},{8,9},{10,11},{12,13},{14,15},{16,17},{18,... | collective-permute-start | bytes 221192 | tf_op jit(solution)/shard_map/ppermute | solution.py:14
  84.3 1.5 fusion.55
  85.8 1.3 reshape.171
  93.3 1.4 fusion.53
  94.8 3.6 %all-reduce.3 = (f32[64]{0:T(128)S(1)}, f32[64]{0:T(128)S(1)}) all-reduce(f32[64]{0:T(128)S(1)} %get-tuple-element.36, f32[64]{0:T(128)S(1)} %get-tuple-element.35), channel_id=1, replica_groups=mesh['dp'=16,'space'=2] {'space'}, use_global_device_ids=true, to_apply=%region_23.24 | all-reduce | flops 128 | bytes 1024 | tf_op jit(solution)/shard_map/psum | solution.py:43
  98.4 1.4 multiply_convert_fusion.2
  99.9 1.6 fusion.5
  101.7 6.3 %concatenate.28 = bf16[70400]{0:T(1024)(128)(2,1)} concatenate(bf16[16384]{0:T(1024)(128)(2,1)S(1)} %reshape.180, bf16[36864]{0:T(1024)(128)(2,1)S(1)} %copy-done.27, bf16[16384]{0:T(1024)(128)(2,1)S(1)} %bitcast.206, bf16[64]{0:T(256)(128)(2,1)S(1)} %convert.77, bf16[64]{0:T(256)(128)(2,1)S(1)} %convert.78, bf16[64]{0:T(256)(128)(2,1)S(1)} %copy-done.39, ...), dimensions={0} | concatenate | bytes 281600 | tf_op jit(solution)/shard_map/concatenate | solution.py:137
  108.1 1.5 fusion
  109.6 18.9 %all-reduce.9.cloned.1.call-done = bf16[70400]{0:T(1024)(128)(2,1)} async-done(((bf16[70400]{0:T(1024)(128)(2,1)}), bf16[70400]{0:T(1024)(128)(2,1)}) %all-reduce.9.cloned.1.call-update) | async-done | bytes 140816
  129.5 78.9 %all-reduce.10 = bf16[35200]{0:T(1024)(128)(2,1)S(1)} all-reduce(f32[35200]{0:T(1024)S(1)} %dynamic-slice_convert_fusion), channel_id=1, replica_groups=mesh['dp'=16,'space'=2] {'dp'}, use_global_device_ids=true, to_apply=%region_25.26 | all-reduce | flops 35200 | bytes 211200 | tf_op jit(solution)/shard_map/psum | solution.py:145
  208.5 2.0 all-gather
  (187 shorter events, 40.8 us)
Async XLA Ops:
  7.2 41.0 %copy-start = (bf16[64,256]{1,0:T(8,128)(2,1)S(1)}, bf16[64,256]{1,0:T(8,128)(2,1)}, u32[]{:S(2)}) copy-start(bf16[64,256]{1,0:T(8,128)(2,1)} %param.14) | copy-start | bytes 98308
  7.2 13.4 %copy-start.45 = (u32[32]{0:T(128)S(1)}, u32[32]{0:T(128)}, u32[]{:S(2)}) copy-start(u32[32]{0:T(128)} %constant.51) | copy-start | bytes 388
  7.2 7.3 %copy-start.34 = (f32[64]{0:T(128)S(1)}, f32[64]{0:T(128)}, u32[]{:S(2)}) copy-start(f32[64]{0:T(128)} %param.15) | copy-start | bytes 772
  7.2 8.4 %copy-start.37 = (f32[64]{0:T(128)S(1)}, f32[64]{0:T(128)}, u32[]{:S(2)}) copy-start(f32[64]{0:T(128)} %param.16) | copy-start | bytes 772
  7.2 14.6 %copy-start.25 = (bf16[3,3,64,64]{3,2,1,0:T(8,128)(2,1)S(1)}, bf16[3,3,64,64]{3,2,1,0:T(8,128)(2,1)}, u32[]{:S(2)}) copy-start(bf16[3,3,64,64]{3,2,1,0:T(8,128)(2,1)} %param.13) | copy-start | bytes 221188
  7.2 121.3 %all-reduce.9.cloned.1.call-start = ((), (), s32[]{:S(2)}) async-start(), calls=%async_computation | async-start | bytes 282624
  16.3 6.3 %collective-permute-start = (bf16[2,288,64]{1,0,2:T(2,128)(2,1)S(1)}, bf16[2,288,64]{1,0,2:T(2,128)(2,1)S(1)}, u32[]{:S(2)}, u32[]{:S(2)}) collective-permute-start(bf16[2,288,64]{1,0,2:T(2,128)(2,1)S(1)} %slice.191), channel_id=1, source_target_pairs={{0,1},{2,3},{4,5},{6,7},{8,9},{10,11},{12,13},{14,15},{16,17},{18,... | collective-permute-start | bytes 221192 | tf_op jit(solution)/shard_map/ppermute | solution.py:14
  18.7 3.9 %collective-permute-start.1 = (bf16[2,288,64]{1,0,2:T(2,128)(2,1)S(1)}, bf16[2,288,64]{1,0,2:T(2,128)(2,1)S(1)}, u32[]{:S(2)}, u32[]{:S(2)}) collective-permute-start(bf16[2,288,64]{1,0,2:T(2,128)(2,1)S(1)} %slice.193), channel_id=1, source_target_pairs={{1,0},{3,2},{5,4},{7,6},{9,8},{11,10},{13,12},{15,14},{17,16},{19,... | collective-permute-start | bytes 221192 | tf_op jit(solution)/shard_map/ppermute | solution.py:17
  25.7 5.7 %copy-start.9 = (bf16[2304,64]{0,1:T(8,128)(2,1)}, bf16[2304,64]{0,1:T(8,128)(2,1)S(1)}, u32[]{:S(2)}) copy-start(bf16[2304,64]{0,1:T(8,128)(2,1)S(1)} %reshape.161) | copy-start | bytes 884740
  27.5 6.1 %copy-start.15 = (bf16[2304,64]{0,1:T(8,128)(2,1)}, bf16[2304,64]{0,1:T(8,128)(2,1)S(1)}, u32[]{:S(2)}) copy-start(bf16[2304,64]{0,1:T(8,128)(2,1)S(1)} %reshape.162) | copy-start | bytes 884740
  28.9 4.6 %copy-start.13 = (bf16[2304,64]{0,1:T(8,128)(2,1)}, bf16[2304,64]{0,1:T(8,128)(2,1)S(1)}, u32[]{:S(2)}) copy-start(bf16[2304,64]{0,1:T(8,128)(2,1)S(1)} %reshape.163) | copy-start | bytes 884740
  35.9 5.2 %copy-start.19 = (bf16[2304,64]{0,1:T(8,128)(2,1)}, bf16[2304,64]{0,1:T(8,128)(2,1)S(1)}, u32[]{:S(2)}) copy-start(bf16[2304,64]{0,1:T(8,128)(2,1)S(1)} %reshape.165) | copy-start | bytes 884740
  40.0 8.2 %copy-start.43 = (f32[64]{0:T(128)S(1)}, f32[64]{0:T(128)}, u32[]{:S(2)}) copy-start(f32[64]{0:T(128)} %param.17) | copy-start | bytes 772
  40.0 8.2 %copy-start.44 = (f32[64]{0:T(128)S(1)}, f32[64]{0:T(128)}, u32[]{:S(2)}) copy-start(f32[64]{0:T(128)} %param.18) | copy-start | bytes 772
  42.2 6.0 %copy-start.2 = (f32[2304,64]{0,1:T(8,128)}, f32[2304,64]{0,1:T(8,128)S(1)}, u32[]{:S(2)}) copy-start(f32[2304,64]{0,1:T(8,128)S(1)} %get-tuple-element.84) | copy-start | bytes 1769476
  48.2 7.4 %copy-start.33 = (f32[256]{0:T(256)S(1)}, f32[256]{0:T(256)}, u32[]{:S(2)}) copy-start(f32[256]{0:T(256)} %param.19) | copy-start | bytes 3076
  48.2 7.4 %copy-start.36 = (f32[256]{0:T(256)S(1)}, f32[256]{0:T(256)}, u32[]{:S(2)}) copy-start(f32[256]{0:T(256)} %param.20) | copy-start | bytes 3076
  65.8 5.6 %copy-start.10 = (bf16[2304,64]{0,1:T(8,128)(2,1)S(1)}, bf16[2304,64]{0,1:T(8,128)(2,1)}, u32[]{:S(2)}) copy-start(bf16[2304,64]{0,1:T(8,128)(2,1)} %copy-done.9) | copy-start | bytes 884740
  67.3 4.5 %copy-start.16 = (bf16[2304,64]{0,1:T(8,128)(2,1)S(1)}, bf16[2304,64]{0,1:T(8,128)(2,1)}, u32[]{:S(2)}) copy-start(bf16[2304,64]{0,1:T(8,128)(2,1)} %copy-done.15) | copy-start | bytes 884740
  67.3 4.7 %copy-start.14 = (bf16[2304,64]{0,1:T(8,128)(2,1)S(1)}, bf16[2304,64]{0,1:T(8,128)(2,1)}, u32[]{:S(2)}) copy-start(bf16[2304,64]{0,1:T(8,128)(2,1)} %copy-done.13) | copy-start | bytes 884740
  67.3 5.0 %copy-start.12 = (bf16[2304,64]{0,1:T(8,128)(2,1)S(1)}, bf16[2304,64]{0,1:T(8,128)(2,1)}, u32[]{:S(2)}) copy-start(bf16[2304,64]{0,1:T(8,128)(2,1)} %copy-done.11) | copy-start | bytes 884740
  71.8 5.6 %copy-start.8 = (bf16[2304,64]{0,1:T(8,128)(2,1)S(1)}, bf16[2304,64]{0,1:T(8,128)(2,1)}, u32[]{:S(2)}) copy-start(bf16[2304,64]{0,1:T(8,128)(2,1)} %copy-done.7) | copy-start | bytes 884740
  73.6 7.4 %collective-permute-start.2 = (bf16[2,288,64]{1,0,2:T(2,128)(2,1)S(1)}, bf16[2,288,64]{1,0,2:T(2,128)(2,1)S(1)}, u32[]{:S(2)}, u32[]{:S(2)}) collective-permute-start(bf16[2,288,64]{1,0,2:T(2,128)(2,1)S(1)} %slice.212), channel_id=1, source_target_pairs={{0,1},{2,3},{4,5},{6,7},{8,9},{10,11},{12,13},{14,15},{16,17},{18,... | collective-permute-start | bytes 221192 | tf_op jit(solution)/shard_map/ppermute | solution.py:14
  76.0 5.0 %collective-permute-start.3 = (bf16[2,288,64]{1,0,2:T(2,128)(2,1)S(1)}, bf16[2,288,64]{1,0,2:T(2,128)(2,1)S(1)}, u32[]{:S(2)}, u32[]{:S(2)}) collective-permute-start(bf16[2,288,64]{1,0,2:T(2,128)(2,1)S(1)} %slice.214), channel_id=1, source_target_pairs={{1,0},{3,2},{5,4},{7,6},{9,8},{11,10},{13,12},{15,14},{17,16},{19,... | collective-permute-start | bytes 221192 | tf_op jit(solution)/shard_map/ppermute | solution.py:17
  84.2 4.9 %copy-start.26 = (bf16[3,3,64,64]{2,3,1,0:T(8,128)(2,1)S(1)}, bf16[3,3,64,64]{2,3,1,0:T(8,128)(2,1)}, u32[]{:S(2)}) copy-start(bf16[3,3,64,64]{2,3,1,0:T(8,128)(2,1)} %reverse_bitcast_fusion) | copy-start | bytes 221188
  94.7 7.0 %copy-start.27 = (bf16[36864]{0:T(1024)(128)(2,1)S(1)}, bf16[36864]{0:T(1024)(128)(2,1)}, u32[]{:S(2)}) copy-start(bf16[36864]{0:T(1024)(128)(2,1)} %reshape_reshape.4) | copy-start | bytes 221188
  94.7 7.0 %copy-start.39 = (bf16[64]{0:T(256)(128)(2,1)S(1)}, bf16[64]{0:T(256)(128)(2,1)}, u32[]{:S(2)}) copy-start(bf16[64]{0:T(256)(128)(2,1)} %convert.79) | copy-start | bytes 388
  94.7 7.0 %copy-start.40 = (bf16[64]{0:T(256)(128)(2,1)S(1)}, bf16[64]{0:T(256)(128)(2,1)}, u32[]{:S(2)}) copy-start(bf16[64]{0:T(256)(128)(2,1)} %convert.80) | copy-start | bytes 388
  94.7 7.0 %copy-start.41 = (bf16[256]{0:T(256)(128)(2,1)S(1)}, bf16[256]{0:T(256)(128)(2,1)}, u32[]{:S(2)}) copy-start(bf16[256]{0:T(256)(128)(2,1)} %convert.81) | copy-start | bytes 1540
  94.8 7.0 %copy-start.42 = (bf16[256]{0:T(256)(128)(2,1)S(1)}, bf16[256]{0:T(256)(128)(2,1)}, u32[]{:S(2)}) copy-start(bf16[256]{0:T(256)(128)(2,1)} %convert.82) | copy-start | bytes 1540
  94.8 13.3 %copy-start.1 = (f32[2304,256]{1,0:T(8,128)S(1)}, f32[2304,256]{1,0:T(8,128)}, u32[]{:S(2)}) copy-start(f32[2304,256]{1,0:T(8,128)} %get-tuple-element.45) | copy-start | bytes 7077892
  94.8 13.3 %copy-start.28 = (bf16[256,64]{0,1:T(8,128)(2,1)S(1)}, bf16[256,64]{0,1:T(8,128)(2,1)}, u32[]{:S(2)}) copy-start(bf16[256,64]{0,1:T(8,128)(2,1)} %param.12) | copy-start | bytes 98308
  (19 other events, 45.6 us)
Sparse Core Ops, SparseCore 0:
  108.2 20.3 all-reduce.8
where the time goes:
time: 223 us; the launch traced here: 222 us
  blocking collectives  106 us (48%)
  local copies, waits for them, and re-layouts  29.5 us (13%)
  matrix products  23.4 us (10%)
  other arithmetic  21.6 us (10%)
  waiting for transfers between devices  19 us (9%)
  between operations  15.8 us (7%)
  starting transfers between devices  7.13 us (3%)
    psum x1, blocking collectives, shards(): share = lax.psum(share, 'dp')  78.9 us
    unnamed x2, waiting for transfers between devices  19 us
    dot_general x18, matrix products, dilated(): jnp.dot(window, kernel[tap_row, tap_col], preferred_element_type=jnp.floa...  12.7 us
    reshape x16, local copies, waits for them, and re-layouts, dilated(): window = padded[2 * tap_row:2 * tap_row + rows, 2 * tap_col:2 * tap_col +...  12.4 us
    psum x3, blocking collectives, backnorm(): grad_sum, grad_cross = lax.psum((local_sum, local_cross), 'space')  8.68 us
    psum x3, blocking collectives, normalize(): average = lax.psum(jnp.sum(pre, 0), 'space') / count  8.36 us
    psum x3, blocking collectives, normalize(): variance = lax.psum(jnp.sum(centred * centred, 0), 'space') / count  7.59 us
    concatenate x1, local copies, waits for them, and re-layouts, shards(): flat_grads = jnp.concatenate([item.reshape(-1) for item in parts_list])  6.29 us
  transfers between devices with their start and end apart: 5, of which 1 were waited for; matrix products, arithmetic and copies ran while one was open for 3% of the time, Pallas kernels for 0%

commit v1 on v0

--- a/solution.py
+++ b/solution.py
@@ -142,7 +142,7 @@
     share = lax.psum_scatter(
         flat_grads.astype(jnp.bfloat16), "space", scatter_dimension=0, tiled=True
     ).astype(jnp.float32)
-    share = lax.psum(share, "dp")
+    share = jnp.sum(lax.all_gather(share, "dp"), axis=0)
     whole = lax.all_gather(share.astype(jnp.bfloat16), "space", axis=0, tiled=True).astype(
         share.dtype
     )

time: 223 us -> 212 us (0.951)
  blocking collectives: 106 us -> 25.8 us
  waiting for transfers between devices: 19 us -> 82.5 us
  other arithmetic: 21.6 us -> 24.6 us
    psum x1 -> x0, blocking collectives: 78.9 us -> none  [shards(): share = lax.psum(share, 'dp')]
    all_gather x0 -> x1, waiting for transfers between devices: none -> 62.7 us  [shards(): share = jnp.sum(lax.all_gather(share, 'dp'), axis=0)]
    reduce_sum x0 -> x1, other arithmetic: none -> 3.03 us  [shards(): share = jnp.sum(lax.all_gather(share, 'dp'), axis=0)]
    unnamed x2 -> x3, waiting for transfers between devices: 19 us -> 19.2 us
  transfers between devices with their start and end apart: 5 -> 6, of which waited for: 1 -> 3; matrix products, arithmetic and copies ran while one was open for 3% -> 3% of each run, Pallas kernels for 0% -> 0%
where the time goes in v1:
time: 212 us; the launch traced here: 210 us
  waiting for transfers between devices  82.5 us (39%)
  local copies, waits for them, and re-layouts  31.1 us (15%)
  blocking collectives  25.8 us (12%)
  other arithmetic  24.6 us (12%)
  matrix products  23.4 us (11%)
  between operations  15.8 us (7%)
  starting transfers between devices  7.17 us (3%)
    all_gather x1, waiting for transfers between devices, shards(): share = jnp.sum(lax.all_gather(share, 'dp'), axis=0)  62.7 us
    unnamed x3, waiting for transfers between devices  19.2 us
    reshape x16, local copies, waits for them, and re-layouts, dilated(): window = padded[2 * tap_row:2 * tap_row + rows, 2 * tap_col:2 * tap_col +...  13.2 us
    dot_general x18, matrix products, dilated(): jnp.dot(window, kernel[tap_row, tap_col], preferred_element_type=jnp.floa...  12.7 us
    psum x3, blocking collectives, backnorm(): grad_sum, grad_cross = lax.psum((local_sum, local_cross), 'space')  8.45 us
    psum x3, blocking collectives, normalize(): average = lax.psum(jnp.sum(pre, 0), 'space') / count  7.77 us
    psum x3, blocking collectives, normalize(): variance = lax.psum(jnp.sum(centred * centred, 0), 'space') / count  7.59 us
    concatenate x1, local copies, waits for them, and re-layouts, shards(): flat_grads = jnp.concatenate([item.reshape(-1) for item in parts_list])  6.29 us
  transfers between devices with their start and end apart: 6, of which 3 were waited for; matrix products, arithmetic and copies ran while one was open for 3% of the time, Pallas kernels for 0%

profile of v1, /device:TPU:0, one launch (start us, length us, event | category | flops | bytes accessed | tf_op | source)
XLA Modules:
  0.0 210.4 jit_solution(5421898446842134675)
XLA Ops:
  7.3 1.9 fusion.59
  9.2 2.6 %psum.84 = f32[64]{0:T(128)S(1)} all-reduce(f32[64]{0:T(128)S(1)} %get-tuple-element.81), channel_id=1, replica_groups=mesh['dp'=16,'space'=2] {'space'}, use_global_device_ids=true, to_apply=%region_1.0 | all-reduce | flops 64 | bytes 512 | tf_op jit(solution)/shard_map/psum | solution.py:32
  12.1 2.5 %psum.85 = f32[64]{0:T(128)S(1)} all-reduce(f32[64]{0:T(128)S(1)} %multiply_reduce_fusion.5), channel_id=1, replica_groups=mesh['dp'=16,'space'=2] {'space'}, use_global_device_ids=true, to_apply=%region_3.0 | all-reduce | flops 64 | bytes 512 | tf_op jit(solution)/shard_map/psum | solution.py:34
  16.3 2.3 %collective-permute-start = (bf16[2,288,64]{1,0,2:T(2,128)(2,1)S(1)}, bf16[2,288,64]{1,0,2:T(2,128)(2,1)S(1)}, u32[]{:S(2)}, u32[]{:S(2)}) collective-permute-start(bf16[2,288,64]{1,0,2:T(2,128)(2,1)S(1)} %slice.191), channel_id=1, source_target_pairs={{0,1},{2,3},{4,5},{6,7},{8,9},{10,11},{12,13},{14,15},{16,17},{18,... | collective-permute-start | bytes 221192 | tf_op jit(solution)/shard_map/ppermute | solution.py:14
  22.9 1.8 fusion.56
  26.8 1.4 reshape.163
  28.2 1.4 reshape.164
  34.2 1.4 reshape.166
  37.0 1.3 reshape.167
  41.6 2.7 %psum.86 = f32[64]{0:T(128)S(1)} all-reduce(f32[64]{0:T(128)S(1)} %get-tuple-element.83), channel_id=1, replica_groups=mesh['dp'=16,'space'=2] {'space'}, use_global_device_ids=true, to_apply=%region_5.6 | all-reduce | flops 64 | bytes 512 | tf_op jit(solution)/shard_map/psum | solution.py:32
  44.5 2.5 %psum.87 = f32[64]{0:T(128)S(1)} all-reduce(f32[64]{0:T(128)S(1)} %multiply_reduce_fusion.4), channel_id=1, replica_groups=mesh['dp'=16,'space'=2] {'space'}, use_global_device_ids=true, to_apply=%region_7.8 | all-reduce | flops 64 | bytes 512 | tf_op jit(solution)/shard_map/psum | solution.py:34
  47.1 1.9 fusion.61
  48.9 2.5 %psum.88 = f32[256]{0:T(256)S(1)} all-reduce(f32[256]{0:T(256)S(1)} %get-tuple-element.85), channel_id=1, replica_groups=mesh['dp'=16,'space'=2] {'space'}, use_global_device_ids=true, to_apply=%region_9.10 | all-reduce | flops 256 | bytes 2048 | tf_op jit(solution)/shard_map/psum | solution.py:32
  51.8 2.6 %psum.89 = f32[256]{0:T(256)S(1)} all-reduce(f32[256]{0:T(256)S(1)} %multiply_reduce_fusion.1), channel_id=1, replica_groups=mesh['dp'=16,'space'=2] {'space'}, use_global_device_ids=true, to_apply=%region_11.12 | all-reduce | flops 256 | bytes 2048 | tf_op jit(solution)/shard_map/psum | solution.py:34
  54.4 5.1 %fusion.52 = (f32[256]{0:T(256)S(1)}, f32[256]{0:T(256)S(1)}, f32[2304,256]{1,0:T(8,128)}, bf16[2304,256]{1,0:T(8,128)(2,1)}) fusion(f32[256]{0:T(256)S(1)} %get-tuple-element.76, f32[2304,256]{1,0:T(8,128)S(1)} %get-tuple-element.86, f32[256]{0:T(256)S(1)} %broadcast_multiply_fusion.1, bf16[1,8,288,256]{3,2,1,0:T(8,128)(2,1)} %param.11, ...), kind=kLoop, calls=%fused_computation.141 | loop fusion | flops 11795968 | bytes 8263680 | tf_op jit(solution)/shard_map/reduce_sum | solution.py:41
  59.5 2.5 %all-reduce.5 = (f32[256]{0:T(256)S(1)}, f32[256]{0:T(256)S(1)}) all-reduce(f32[256]{0:T(256)S(1)} %get-tuple-element.34, f32[256]{0:T(256)S(1)} %get-tuple-element.33), channel_id=1, replica_groups=mesh['dp'=16,'space'=2] {'space'}, use_global_device_ids=true, to_apply=%region_15.16 | all-reduce | flops 512 | bytes 4096 | tf_op jit(solution)/shard_map/psum | solution.py:43
  61.9 2.3 %multiply_convert_fusion = bf16[2304,256]{1,0:T(8,128)(2,1)S(1)} fusion(f32[2304,256]{1,0:T(8,128)} %get-tuple-element.45, f32[2304,256]{1,0:T(8,128)S(1)} %get-tuple-element.86, f32[256]{0:T(256)S(1)} %get-tuple-element.43, f32[256]{0:T(256)S(1)} %broadcast_multiply_fusion, f32[256]{0:T(256)S(1)} %get-tuple-element.75, f32[256]{0:T(256)S(1)} %get-tuple-element.76, ...), kind=kLoop, calls=%fused_computation.23 | loop fusion | flops 4718592 | bytes 5903360 | tf_op jit(solution)/shard_map/convert_element_type | solution.py:44
  64.7 1.5 fusion.54
  66.2 2.6 %all-reduce.4 = (f32[64]{0:T(128)S(1)}, f32[64]{0:T(128)S(1)}) all-reduce(f32[64]{0:T(128)S(1)} %get-tuple-element.38, f32[64]{0:T(128)S(1)} %get-tuple-element.37), channel_id=1, replica_groups=mesh['dp'=16,'space'=2] {'space'}, use_global_device_ids=true, to_apply=%region_19.20 | all-reduce | flops 128 | bytes 1024 | tf_op jit(solution)/shard_map/psum | solution.py:43
  68.8 1.5 multiply_convert_fusion.3
  72.5 2.3 %collective-permute-start.2 = (bf16[2,288,64]{1,0,2:T(2,128)(2,1)S(1)}, bf16[2,288,64]{1,0,2:T(2,128)(2,1)S(1)}, u32[]{:S(2)}, u32[]{:S(2)}) collective-permute-start(bf16[2,288,64]{1,0,2:T(2,128)(2,1)S(1)} %slice.212), channel_id=1, source_target_pairs={{0,1},{2,3},{4,5},{6,7},{8,9},{10,11},{12,13},{14,15},{16,17},{18,... | collective-permute-start | bytes 221192 | tf_op jit(solution)/shard_map/ppermute | solution.py:14
  83.1 1.5 fusion.55
  92.9 1.4 fusion.53
  94.3 3.4 %all-reduce.3 = (f32[64]{0:T(128)S(1)}, f32[64]{0:T(128)S(1)}) all-reduce(f32[64]{0:T(128)S(1)} %get-tuple-element.36, f32[64]{0:T(128)S(1)} %get-tuple-element.35), channel_id=1, replica_groups=mesh['dp'=16,'space'=2] {'space'}, use_global_device_ids=true, to_apply=%region_23.24 | all-reduce | flops 128 | bytes 1024 | tf_op jit(solution)/shard_map/psum | solution.py:43
  97.7 1.4 multiply_convert_fusion.2
  99.2 1.6 fusion.5
  101.1 6.3 %concatenate.28 = bf16[70400]{0:T(1024)(128)(2,1)} concatenate(bf16[16384]{0:T(1024)(128)(2,1)S(1)} %reshape.180, bf16[36864]{0:T(1024)(128)(2,1)S(1)} %copy-done.27, bf16[16384]{0:T(1024)(128)(2,1)S(1)} %bitcast.206, bf16[64]{0:T(256)(128)(2,1)S(1)} %convert.78, bf16[64]{0:T(256)(128)(2,1)S(1)} %convert.79, bf16[64]{0:T(256)(128)(2,1)S(1)} %copy-done.40, ...), dimensions={0} | concatenate | bytes 281600 | tf_op jit(solution)/shard_map/concatenate | solution.py:137
  108.7 19.2 %all-reduce.8.cloned.1.call-done = bf16[70400]{0:T(1024)(128)(2,1)} async-done(((bf16[70400]{0:T(1024)(128)(2,1)}), bf16[70400]{0:T(1024)(128)(2,1)}) %all-reduce.8.cloned.1.call-update) | async-done | bytes 140816
  129.7 1.5 fusion
  131.2 62.7 %all-gather.5.cloned.1.call-done = f32[16,1,35200]{2,1,0:T(1,128)} async-done(((f32[1,1,35200]{2,1,0:T(1,128)}), f32[16,1,35200]{2,1,0:T(1,128)}) %all-gather.5.cloned.1.call-update) | async-done | bytes 2252816 | tf_op jit(solution)/shard_map/all_gather | solution.py:145
  193.9 3.0 %reduce_sum.129 = bf16[35200]{0:T(1024)(128)(2,1)S(1)} reduce(f32[16,1,35200]{2,1,0:T(1,128)} %all-gather.5.cloned.1.call-done, f32[]{:T(128)} %constant.37.clone.1), dimensions={0,1}, to_apply=%region_25.26 | reduce | flops 528000 | bytes 2323204 | tf_op jit(solution)/shard_map/reduce_sum | solution.py:145
  197.0 2.0 all-gather.2
  (193 shorter events, 44.2 us)
Async XLA Ops:
  7.2 39.9 %copy-start = (bf16[64,256]{1,0:T(8,128)(2,1)S(1)}, bf16[64,256]{1,0:T(8,128)(2,1)}, u32[]{:S(2)}) copy-start(bf16[64,256]{1,0:T(8,128)(2,1)} %param.14) | copy-start | bytes 98308
  7.2 7.3 %copy-start.35 = (f32[64]{0:T(128)S(1)}, f32[64]{0:T(128)}, u32[]{:S(2)}) copy-start(f32[64]{0:T(128)} %param.15) | copy-start | bytes 772
  7.2 8.4 %copy-start.38 = (f32[64]{0:T(128)S(1)}, f32[64]{0:T(128)}, u32[]{:S(2)}) copy-start(f32[64]{0:T(128)} %param.16) | copy-start | bytes 772
  7.2 13.4 %copy-start.25 = (bf16[3,3,64,64]{3,2,1,0:T(8,128)(2,1)S(1)}, bf16[3,3,64,64]{3,2,1,0:T(8,128)(2,1)}, u32[]{:S(2)}) copy-start(bf16[3,3,64,64]{3,2,1,0:T(8,128)(2,1)} %param.13) | copy-start | bytes 221188
  7.2 120.6 %all-reduce.8.cloned.1.call-start = ((), (), s32[]{:S(2)}) async-start(), calls=%async_computation.1 | async-start | bytes 282624
  16.3 5.0 %collective-permute-start = (bf16[2,288,64]{1,0,2:T(2,128)(2,1)S(1)}, bf16[2,288,64]{1,0,2:T(2,128)(2,1)S(1)}, u32[]{:S(2)}, u32[]{:S(2)}) collective-permute-start(bf16[2,288,64]{1,0,2:T(2,128)(2,1)S(1)} %slice.191), channel_id=1, source_target_pairs={{0,1},{2,3},{4,5},{6,7},{8,9},{10,11},{12,13},{14,15},{16,17},{18,... | collective-permute-start | bytes 221192 | tf_op jit(solution)/shard_map/ppermute | solution.py:14
  18.7 3.2 %collective-permute-start.1 = (bf16[2,288,64]{1,0,2:T(2,128)(2,1)S(1)}, bf16[2,288,64]{1,0,2:T(2,128)(2,1)S(1)}, u32[]{:S(2)}, u32[]{:S(2)}) collective-permute-start(bf16[2,288,64]{1,0,2:T(2,128)(2,1)S(1)} %slice.193), channel_id=1, source_target_pairs={{1,0},{3,2},{5,4},{7,6},{9,8},{11,10},{13,12},{15,14},{17,16},{19,... | collective-permute-start | bytes 221192 | tf_op jit(solution)/shard_map/ppermute | solution.py:17
  25.0 5.7 %copy-start.9 = (bf16[2304,64]{0,1:T(8,128)(2,1)}, bf16[2304,64]{0,1:T(8,128)(2,1)S(1)}, u32[]{:S(2)}) copy-start(bf16[2304,64]{0,1:T(8,128)(2,1)S(1)} %reshape.161) | copy-start | bytes 884740
  26.8 6.1 %copy-start.15 = (bf16[2304,64]{0,1:T(8,128)(2,1)}, bf16[2304,64]{0,1:T(8,128)(2,1)S(1)}, u32[]{:S(2)}) copy-start(bf16[2304,64]{0,1:T(8,128)(2,1)S(1)} %reshape.162) | copy-start | bytes 884740
  28.2 4.6 %copy-start.13 = (bf16[2304,64]{0,1:T(8,128)(2,1)}, bf16[2304,64]{0,1:T(8,128)(2,1)S(1)}, u32[]{:S(2)}) copy-start(bf16[2304,64]{0,1:T(8,128)(2,1)S(1)} %reshape.163) | copy-start | bytes 884740
  34.2 6.3 %copy-start.19 = (bf16[2304,64]{0,1:T(8,128)(2,1)}, bf16[2304,64]{0,1:T(8,128)(2,1)S(1)}, u32[]{:S(2)}) copy-start(bf16[2304,64]{0,1:T(8,128)(2,1)S(1)} %reshape.165) | copy-start | bytes 884740
  39.4 7.6 %copy-start.44 = (f32[64]{0:T(128)S(1)}, f32[64]{0:T(128)}, u32[]{:S(2)}) copy-start(f32[64]{0:T(128)} %param.17) | copy-start | bytes 772
  39.4 7.6 %copy-start.45 = (f32[64]{0:T(128)S(1)}, f32[64]{0:T(128)}, u32[]{:S(2)}) copy-start(f32[64]{0:T(128)} %param.18) | copy-start | bytes 772
  41.6 5.4 %copy-start.2 = (f32[2304,64]{0,1:T(8,128)}, f32[2304,64]{0,1:T(8,128)S(1)}, u32[]{:S(2)}) copy-start(f32[2304,64]{0,1:T(8,128)S(1)} %get-tuple-element.84) | copy-start | bytes 1769476
  47.0 7.4 %copy-start.34 = (f32[256]{0:T(256)S(1)}, f32[256]{0:T(256)}, u32[]{:S(2)}) copy-start(f32[256]{0:T(256)} %param.19) | copy-start | bytes 3076
  47.1 7.4 %copy-start.37 = (f32[256]{0:T(256)S(1)}, f32[256]{0:T(256)}, u32[]{:S(2)}) copy-start(f32[256]{0:T(256)} %param.20) | copy-start | bytes 3076
  64.7 5.6 %copy-start.10 = (bf16[2304,64]{0,1:T(8,128)(2,1)S(1)}, bf16[2304,64]{0,1:T(8,128)(2,1)}, u32[]{:S(2)}) copy-start(bf16[2304,64]{0,1:T(8,128)(2,1)} %copy-done.9) | copy-start | bytes 884740
  66.2 4.7 %copy-start.14 = (bf16[2304,64]{0,1:T(8,128)(2,1)S(1)}, bf16[2304,64]{0,1:T(8,128)(2,1)}, u32[]{:S(2)}) copy-start(bf16[2304,64]{0,1:T(8,128)(2,1)} %copy-done.13) | copy-start | bytes 884740
  66.2 5.0 %copy-start.12 = (bf16[2304,64]{0,1:T(8,128)(2,1)S(1)}, bf16[2304,64]{0,1:T(8,128)(2,1)}, u32[]{:S(2)}) copy-start(bf16[2304,64]{0,1:T(8,128)(2,1)} %copy-done.11) | copy-start | bytes 884740
  70.6 5.5 %copy-start.8 = (bf16[2304,64]{0,1:T(8,128)(2,1)S(1)}, bf16[2304,64]{0,1:T(8,128)(2,1)}, u32[]{:S(2)}) copy-start(bf16[2304,64]{0,1:T(8,128)(2,1)} %copy-done.7) | copy-start | bytes 884740
  72.5 7.4 %collective-permute-start.2 = (bf16[2,288,64]{1,0,2:T(2,128)(2,1)S(1)}, bf16[2,288,64]{1,0,2:T(2,128)(2,1)S(1)}, u32[]{:S(2)}, u32[]{:S(2)}) collective-permute-start(bf16[2,288,64]{1,0,2:T(2,128)(2,1)S(1)} %slice.212), channel_id=1, source_target_pairs={{0,1},{2,3},{4,5},{6,7},{8,9},{10,11},{12,13},{14,15},{16,17},{18,... | collective-permute-start | bytes 221192 | tf_op jit(solution)/shard_map/ppermute | solution.py:14
  74.9 5.0 %collective-permute-start.3 = (bf16[2,288,64]{1,0,2:T(2,128)(2,1)S(1)}, bf16[2,288,64]{1,0,2:T(2,128)(2,1)S(1)}, u32[]{:S(2)}, u32[]{:S(2)}) collective-permute-start(bf16[2,288,64]{1,0,2:T(2,128)(2,1)S(1)} %slice.214), channel_id=1, source_target_pairs={{1,0},{3,2},{5,4},{7,6},{9,8},{11,10},{13,12},{15,14},{17,16},{19,... | collective-permute-start | bytes 221192 | tf_op jit(solution)/shard_map/ppermute | solution.py:17
  83.1 5.0 %copy-start.26 = (bf16[3,3,64,64]{2,3,1,0:T(8,128)(2,1)S(1)}, bf16[3,3,64,64]{2,3,1,0:T(8,128)(2,1)}, u32[]{:S(2)}) copy-start(bf16[3,3,64,64]{2,3,1,0:T(8,128)(2,1)} %reverse_bitcast_fusion) | copy-start | bytes 221188
  94.2 6.8 %copy-start.27 = (bf16[36864]{0:T(1024)(128)(2,1)S(1)}, bf16[36864]{0:T(1024)(128)(2,1)}, u32[]{:S(2)}) copy-start(bf16[36864]{0:T(1024)(128)(2,1)} %reshape_reshape.4) | copy-start | bytes 221188
  94.3 6.8 %copy-start.40 = (bf16[64]{0:T(256)(128)(2,1)S(1)}, bf16[64]{0:T(256)(128)(2,1)}, u32[]{:S(2)}) copy-start(bf16[64]{0:T(256)(128)(2,1)} %convert.80) | copy-start | bytes 388
  94.3 6.8 %copy-start.41 = (bf16[64]{0:T(256)(128)(2,1)S(1)}, bf16[64]{0:T(256)(128)(2,1)}, u32[]{:S(2)}) copy-start(bf16[64]{0:T(256)(128)(2,1)} %convert.81) | copy-start | bytes 388
  94.3 6.8 %copy-start.42 = (bf16[256]{0:T(256)(128)(2,1)S(1)}, bf16[256]{0:T(256)(128)(2,1)}, u32[]{:S(2)}) copy-start(bf16[256]{0:T(256)(128)(2,1)} %convert.82) | copy-start | bytes 1540
  94.3 6.8 %copy-start.43 = (bf16[256]{0:T(256)(128)(2,1)S(1)}, bf16[256]{0:T(256)(128)(2,1)}, u32[]{:S(2)}) copy-start(bf16[256]{0:T(256)(128)(2,1)} %convert.83) | copy-start | bytes 1540
  94.3 13.1 %copy-start.46 = (u32[32]{0:T(128)S(1)}, u32[32]{0:T(128)}, u32[]{:S(2)}) copy-start(u32[32]{0:T(128)} %constant.51) | copy-start | bytes 388
  94.3 35.3 %copy-start.1 = (f32[2304,256]{1,0:T(8,128)S(1)}, f32[2304,256]{1,0:T(8,128)}, u32[]{:S(2)}) copy-start(f32[2304,256]{1,0:T(8,128)} %get-tuple-element.45) | copy-start | bytes 7077892
  94.3 35.3 %copy-start.29 = (bf16[256,64]{0,1:T(8,128)(2,1)S(1)}, bf16[256,64]{0,1:T(8,128)(2,1)}, u32[]{:S(2)}) copy-start(bf16[256,64]{0,1:T(8,128)(2,1)} %param.12) | copy-start | bytes 98308
  107.4 86.5 %all-gather.5.cloned.1.call-start = ((), (), s32[]{:S(2)}) async-start(), calls=%async_computation | async-start | bytes 2393600 | tf_op jit(solution)/shard_map/all_gather | solution.py:145
  (21 other events, 50.4 us)
Sparse Core Ops, SparseCore 0:
  107.5 20.3 all-reduce.7
  131.2 62.6 all-gather.4
